TPU v7x, 128 devices: a whole 4x4x4 slice. The times are simulated.
128 devices in a mesh: pipe: 16 (over y_lo, z, core), seq: 8 (over x, y_hi).
Axes of the slice: x: 4, y: 4 (y_hi: 2, y_lo: 2; y = y_hi * 2 + y_lo), z: 4, core: 2. Of those that a mesh axis runs over, the one named last changes fastest.
Arguments:
- x_fwd: float32 [16, 1024, 2048], P('pipe', 'seq'), may hold values from -12 to 12
- x_bwd: float32 [16, 1024, 2048], P('pipe', 'seq'), may hold values from -12 to 12
- grad_in: float32 [16, 1024, 2048], P('pipe', 'seq'), may hold values from -6 to 6
- gain: float32 [16, 2048], P('pipe'), may hold values from 0.25 to 1.75
- w_query: bfloat16 [16, 2048, 2048], P('pipe', None, 'seq'), may hold values from -2 to 2
- w_key: bfloat16 [16, 2048, 2048], P('pipe', None, 'seq'), may hold values from -2 to 2
- w_value: bfloat16 [16, 2048, 2048], P('pipe', None, 'seq'), may hold values from -0.125 to 0.125
- w_out: bfloat16 [16, 2048, 2048], P('pipe', None, 'seq'), may hold values from -0.125 to 0.125
Outputs:
- act_next: float32 [16, 1024, 2048], P('pipe', 'seq')
- grad_prev: float32 [16, 1024, 2048], P('pipe', 'seq')
All inputs are finite; a program needn't handle non-finite values.
Results may differ from a plain program's by a relative error of at most 0.012.
The roundings to bfloat16 on the way count: a program that leaves them out, or rounds other values in their place, can miss the bound.
Values may be sent and summed in bfloat16 or wider, within the bound.
A program may use at most 192 MiB of HBM per device.

v0:
```python
import jax
import jax.numpy as jnp
from jax import lax
from jax.sharding import PartitionSpec as P

HD = 128


def passed_along(value, axis, steps):
    count = lax.axis_size(axis)
    pairs = [(source, (source + steps) % count) for source in range(count)]
    return lax.ppermute(value, axis, pairs)


def rope_tables(positions):
    half_dim = HD // 2
    inverse = 10000.0 ** (-(jnp.arange(half_dim).astype(jnp.float32) * 2.0 / HD))
    angles = positions.astype(jnp.float32)[:, None] * inverse[None, :]
    return (jnp.cos(angles)[:, None, :], jnp.sin(angles)[:, None, :])


def rotate(values, cosine, sine_table):
    shaped = values.reshape(values.shape[0], -1, HD)
    first_half = shaped[..., : HD // 2]
    second_half = shaped[..., HD // 2 :]
    output = jnp.concatenate(
        [
            first_half * cosine - second_half * sine_table,
            second_half * cosine + first_half * sine_table,
        ],
        -1,
    )
    return output.reshape(values.shape)


def rotate_back(values, cosine, sine_table):
    shaped = values.reshape(values.shape[0], -1, HD)
    first_half = shaped[..., : HD // 2]
    second_half = shaped[..., HD // 2 :]
    output = jnp.concatenate(
        [
            first_half * cosine + second_half * sine_table,
            second_half * cosine - first_half * sine_table,
        ],
        -1,
    )
    return output.reshape(values.shape)


def normalize(inputs, gain_row):
    inv_rms = lax.rsqrt(jnp.mean(inputs * inputs, -1, keepdims=True) + 1e-05)
    return ((inputs * inv_rms * gain_row).astype(jnp.bfloat16), inv_rms)


def times_t(left, right):
    return lax.dot_general(
        left, right, (((1,), (1,)), ((), ())), preferred_element_type=jnp.float32
    )


def split_heads(values):
    return values.reshape(values.shape[0], -1, HD)


def attend(query, key_rows, value_rows):
    length = query.shape[0]
    score_scale = HD ** (-0.5)
    key_heads = split_heads(key_rows)
    value_heads = split_heads(value_rows)
    query_blocks = split_heads(query).reshape(length // length, length, -1, HD)

    def one_block(query_block):
        scores = (
            jnp.einsum("qhd,khd->hqk", query_block, key_heads, preferred_element_type=jnp.float32)
            * score_scale
        )
        probs = jax.nn.softmax(scores, axis=-1)
        output = jnp.einsum(
            "hqk,khd->qhd",
            probs.astype(jnp.bfloat16),
            value_heads,
            preferred_element_type=jnp.float32,
        )
        return output.astype(jnp.bfloat16)

    return lax.map(one_block, query_blocks).reshape(length, -1)


def attend_back(query, key_rows, value_rows, grad_out, cosine, sine_table):
    length = query.shape[0]
    score_scale = HD ** (-0.5)
    key_heads = split_heads(key_rows)
    value_heads = split_heads(value_rows)
    query_blocks = split_heads(query).reshape(length // length, length, -1, HD)
    grad_blocks = split_heads(grad_out).reshape(length // length, length, -1, HD)

    def step(totals, operands):
        query_block, grad_block = operands
        scores = (
            jnp.einsum("qhd,khd->hqk", query_block, key_heads, preferred_element_type=jnp.float32)
            * score_scale
        )
        probs = jax.nn.softmax(scores, axis=-1)
        value_grad = jnp.einsum(
            "hqk,qhd->khd",
            probs.astype(jnp.bfloat16),
            grad_block,
            preferred_element_type=jnp.float32,
        )
        prob_grad = jnp.einsum(
            "qhd,khd->hqk", grad_block, value_heads, preferred_element_type=jnp.float32
        )
        row_delta = jnp.sum(probs * prob_grad, -1, keepdims=True)
        score_grad = (probs * (prob_grad - row_delta) * score_scale).astype(jnp.bfloat16)
        query_grad = jnp.einsum(
            "hqk,khd->qhd", score_grad, key_heads, preferred_element_type=jnp.float32
        )
        key_grad = jnp.einsum(
            "hqk,qhd->khd", score_grad, query_block, preferred_element_type=jnp.float32
        )
        return ((totals[0] + key_grad, totals[1] + value_grad), query_grad)

    zero_heads = jnp.zeros(key_heads.shape, jnp.float32)
    (key_total, value_total), query_grads = lax.scan(
        step, (zero_heads, zero_heads), (query_blocks, grad_blocks)
    )
    query_grad = rotate_back(query_grads.reshape(length, -1), cosine, sine_table).astype(
        jnp.bfloat16
    )
    key_grad = rotate_back(key_total.reshape(length, -1), cosine, sine_table).astype(jnp.bfloat16)
    return (query_grad, key_grad, value_total.reshape(length, -1).astype(jnp.bfloat16))


def shards(x_fwd, x_bwd, grad_in, gain, w_query, w_key, w_value, w_out):
    act_in = x_fwd[0]
    saved_in = x_bwd[0]
    grad = grad_in[0]
    gain_row = gain[0]
    local_rows = act_in.shape[0]
    length = local_rows * lax.axis_size("seq")
    normed_fwd, inv_fwd = normalize(act_in, gain_row)
    normed_bwd, inv_bwd = normalize(saved_in, gain_row)
    grad_low = grad.astype(jnp.bfloat16)
    full_cos, full_sin = rope_tables(jnp.arange(length))
    all_fwd = lax.all_gather(normed_fwd, "seq", axis=0, tiled=True)
    all_bwd = lax.all_gather(normed_bwd, "seq", axis=0, tiled=True)
    all_grad = lax.all_gather(grad_low, "seq", axis=0, tiled=True)

    def project(normed):
        query = rotate(
            jnp.dot(normed, w_query[0], preferred_element_type=jnp.float32), full_cos, full_sin
        ).astype(jnp.bfloat16)
        key_rows = rotate(
            jnp.dot(normed, w_key[0], preferred_element_type=jnp.float32), full_cos, full_sin
        ).astype(jnp.bfloat16)
        value_rows = jnp.dot(normed, w_value[0], preferred_element_type=jnp.float32).astype(
            jnp.bfloat16
        )
        return (query, key_rows, value_rows)

    attn = attend(*project(all_fwd))
    branch = lax.psum_scatter(
        times_t(attn, w_out[0]).astype(jnp.bfloat16), "seq", scatter_dimension=0, tiled=True
    )
    attn_grad = jnp.dot(all_grad, w_out[0], preferred_element_type=jnp.float32).astype(jnp.bfloat16)
    query_b, key_b, value_b = project(all_bwd)
    query_grad, key_grad, value_grad = attend_back(
        query_b, key_b, value_b, attn_grad, full_cos, full_sin
    )
    d_normed = lax.psum_scatter(
        (
            times_t(query_grad, w_query[0])
            + times_t(key_grad, w_key[0])
            + times_t(value_grad, w_value[0])
        ).astype(jnp.bfloat16),
        "seq",
        scatter_dimension=0,
        tiled=True,
    ).astype(jnp.float32)
    act_out = act_in + branch.astype(jnp.float32)
    gain_grad = d_normed * gain_row
    d_input = inv_bwd * gain_grad - saved_in * inv_bwd * inv_bwd * inv_bwd * jnp.mean(
        saved_in * gain_grad, -1, keepdims=True
    )
    sent_forward = passed_along(act_out.astype(jnp.bfloat16), "pipe", 1).astype(act_out.dtype)
    sent_backward = passed_along((grad + d_input).astype(jnp.bfloat16), "pipe", -1).astype(
        jnp.float32
    )
    return (sent_forward[None], sent_backward[None])


def solution(mesh):
    placed = (
        P("pipe", "seq", None),
        P("pipe", "seq", None),
        P("pipe", "seq", None),
        P("pipe", None),
        P("pipe", None, "seq"),
        P("pipe", None, "seq"),
        P("pipe", None, "seq"),
        P("pipe", None, "seq"),
    )
    return jax.shard_map(
        shards,
        mesh=mesh,
        in_specs=placed,
        out_specs=(P("pipe", "seq", None), P("pipe", "seq", None)),
        check_vma=False,
    )
```

profile of v0, /device:TPU:0, one launch (start us, length us, event | category | flops | bytes accessed | tf_op | source)
XLA Modules:
  0.0 437.1 jit_solution(6163161213774346154)
XLA Ops:
  10.2 2.8 multiply_convert_fusion.1
  13.0 2.1 bitcast_convert_fusion
  20.6 66.6 %all-gather.6.cloned.1.call-done = bf16[1024,2048]{1,0:T(8,128)(2,1)} async-done(((bf16[128,2048]{1,0:T(8,128)(2,1)}), bf16[1024,2048]{1,0:T(8,128)(2,1)}) %all-gather.6.cloned.1.call-update) | async-done | bytes 4194320 | tf_op jit(solution)/shard_map/all_gather | solution.py:146
  87.2 3.8 fusion.14
  91.0 3.8 fusion.12
  96.2 7.3 %fusion.79 = (f32[2,1024]{1,0:T(2,128)S(1)}, f32[2,1024,1024]{1,2,0:T(8,128)}) fusion(bf16[1024,2,64]{0,2,1:T(8,128)(2,1)} %get-tuple-element.38, bf16[1024,2,64]{0,2,1:T(8,128)(2,1)} %get-tuple-element.37, bf16[1024,2,64]{0,2,1:T(8,128)(2,1)} %get-tuple-element.59, bf16[1024,2,64]{0,2,1:T(8,128)(2,1)} %get-tuple-element.60), kind=kOutput, calls=%fused_computation.107 | convolution fusion | flops 545260544 | bytes 9445376 | tf_op jit(solution)/shard_map/while/body/eval_jaxpr/sub | solution.py:103
  103.4 4.3 convolution_convert_fusion.1
  107.7 51.2 %all-gather.8.cloned.1.call-done = bf16[1024,2048]{1,0:T(8,128)(2,1)} async-done(((bf16[128,2048]{1,0:T(8,128)(2,1)}), bf16[1024,2048]{1,0:T(8,128)(2,1)}) %all-gather.8.cloned.1.call-update) | async-done | bytes 4194320 | tf_op jit(solution)/shard_map/all_gather | solution.py:147
  159.0 3.8 convolution_convert_fusion.2
  163.6 4.5 %fusion.81 = f32[2,1024,1024]{1,2,0:T(8,128)} fusion(bf16[1024,2,128]{0,2,1:T(8,128)(2,1)S(1)} %bitcast.110, bf16[1024,2,128]{0,2,1:T(8,128)(2,1)S(1)} %bitcast.112), kind=kOutput, calls=%fused_computation.109 | convolution fusion | flops 536870912 | bytes 9437184 | tf_op jit(solution)/shard_map/while/body/eval_jaxpr/qhd,khd->hqk/dot_general | solution.py:110
  168.2 15.4 %fusion.34 = f32[1024,2,128]{0,2,1:T(8,128)} fusion(f32[2,1024,1024]{1,2,0:T(8,128)} %fusion.81, bf16[1024,2,64]{0,2,1:T(8,128)(2,1)} %get-tuple-element.38, bf16[1024,2,64]{0,2,1:T(8,128)(2,1)} %get-tuple-element.37, f32[2,1024,1024]{1,2,0:T(8,128)} %get-tuple-element.66, f32[2,1024]{1,0:T(2,128)S(1)} %get-tuple-element.65), kind=kOutput, calls=%fused_computation.32 | convolution fusion | flops 552602624 | bytes 18358272 | tf_op jit(solution)/shard_map/while/body/eval_jaxpr/hqk,qhd->khd/dot_general | solution.py:118
  183.6 14.9 %fusion.31 = f32[1024,2,128]{0,2,1:T(8,128)} fusion(f32[2,1024,1024]{1,2,0:T(8,128)} %fusion.81, bf16[1024,2,64]{0,2,1:T(8,128)(2,1)} %get-tuple-element.59, bf16[1024,2,64]{0,2,1:T(8,128)(2,1)} %get-tuple-element.60, f32[2,1024,1024]{1,2,0:T(8,128)} %get-tuple-element.66, f32[2,1024]{1,0:T(2,128)S(1)} %get-tuple-element.65), kind=kOutput, calls=%fused_computation.31 | convolution fusion | flops 552602624 | bytes 18358272 | tf_op jit(solution)/shard_map/while/body/eval_jaxpr/hqk,khd->qhd/dot_general | solution.py:115
  198.5 5.9 %fusion.38 = bf16[2,128,1024]{2,1,0:T(8,128)(2,1)} fusion(bf16[1024,2,128]{0,2,1:T(8,128)(2,1)} %bitcast.111, f32[2,1024,1024]{1,2,0:T(8,128)} %get-tuple-element.66, f32[2,1024]{1,0:T(2,128)S(1)} %get-tuple-element.65), kind=kOutput, calls=%fused_computation.34 | convolution fusion | flops 541327360 | bytes 9445376 | tf_op jit(solution)/shard_map/while/body/eval_jaxpr/hqk,qhd->khd/dot_general | solution.py:104
  204.4 26.3 %all-gather.4.cloned.1.call-done = bf16[1024,2048]{1,0:T(8,128)(2,1)} async-done(((bf16[128,2048]{1,0:T(8,128)(2,1)}), bf16[1024,2048]{1,0:T(8,128)(2,1)}) %all-gather.4.cloned.1.call-update) | async-done | bytes 4194320 | tf_op jit(solution)/shard_map/all_gather | solution.py:145
  230.7 3.9 fusion.16
  234.6 3.8 fusion.18
  243.0 3.4 add_convert_fusion
  246.5 5.2 %fusion.80 = (f32[2,1024]{1,0:T(2,128)S(1)}, f32[2,1024,1024]{1,2,0:T(8,128)}) fusion(bf16[1024,2,64]{0,2,1:T(8,128)(2,1)S(1)} %copy-done.13, bf16[1024,2,64]{0,2,1:T(8,128)(2,1)S(1)} %copy-done.14, bf16[1024,2,64]{0,2,1:T(8,128)(2,1)S(1)} %copy-done.15, bf16[1024,2,64]{0,2,1:T(8,128)(2,1)S(1)} %copy-done.16), kind=kOutput, calls=%fused_computation.108 | convolution fusion | flops 545260544 | bytes 9445376 | tf_op jit(solution)/shard_map/while/body/eval_jaxpr/sub | solution.py:77
  251.7 3.8 convolution_convert_fusion.3
  257.9 3.3 convolution_convert_fusion
  261.2 68.6 %reduce-scatter.5.cloned.1.call-done = bf16[128,2048]{1,0:T(8,128)(2,1)} async-done(((bf16[1024,2048]{1,0:T(8,128)(2,1)}), bf16[128,2048]{1,0:T(8,128)(2,1)}) %reduce-scatter.5.cloned.1.call-update) | async-done | bytes 524304 | tf_op jit(solution)/shard_map/reduce_scatter | solution.py:170
  331.0 2.5 fusion.43
  334.4 83.1 %reduce-scatter.3.cloned.1.call-done = bf16[128,2048]{1,0:T(8,128)(2,1)} async-done(((bf16[1024,2048]{1,0:T(8,128)(2,1)}), bf16[128,2048]{1,0:T(8,128)(2,1)}) %reduce-scatter.3.cloned.1.call-update) | async-done | bytes 524304 | tf_op jit(solution)/shard_map/reduce_scatter | solution.py:162
  419.9 9.6 %collective-permute-done = bf16[128,2048]{1,0:T(8,128)(2,1)S(1)} collective-permute-done((bf16[128,2048]{1,0:T(8,128)(2,1)S(1)}, bf16[128,2048]{1,0:T(8,128)(2,1)S(1)}, u32[]{:S(2)}, u32[]{:S(2)}) %collective-permute-start) | collective-permute-done | bytes 524320 | tf_op jit(solution)/shard_map/ppermute | solution.py:12
  (71 shorter events, 23.2 us)
Async XLA Ops:
  7.2 96.3 %copy-start = (bf16[1,2048,256]{2,1,0:T(8,128)(2,1)S(1)}, bf16[1,2048,256]{2,1,0:T(8,128)(2,1)}, u32[]{:S(2)}) copy-start(bf16[1,2048,256]{2,1,0:T(8,128)(2,1)} %param.14) | copy-start | bytes 3145732
  7.2 8.8 %copy-start.4 = (bf16[1,2048,256]{2,1,0:T(8,128)(2,1)S(1)}, bf16[1,2048,256]{2,1,0:T(8,128)(2,1)}, u32[]{:S(2)}) copy-start(bf16[1,2048,256]{2,1,0:T(8,128)(2,1)} %param.13) | copy-start | bytes 3145732
  7.2 10.2 %copy-start.3 = (bf16[1,2048,256]{2,1,0:T(8,128)(2,1)S(1)}, bf16[1,2048,256]{2,1,0:T(8,128)(2,1)}, u32[]{:S(2)}) copy-start(bf16[1,2048,256]{2,1,0:T(8,128)(2,1)} %param.12) | copy-start | bytes 3145732
  7.2 80.0 %all-gather.6.cloned.1.call-start = ((), (), s32[]{:S(2)}) async-start(), calls=%async_computation.4 | async-start | bytes 4718592 | tf_op jit(solution)/shard_map/all_gather | solution.py:146
  13.0 146.0 %all-gather.8.cloned.1.call-start = ((), (), s32[]{:S(2)}) async-start(), calls=%async_computation.5 | async-start | bytes 4718592 | tf_op jit(solution)/shard_map/all_gather | solution.py:147
  15.1 215.6 %all-gather.4.cloned.1.call-start = ((), (), s32[]{:S(2)}) async-start(), calls=%async_computation.2 | async-start | bytes 4718592 | tf_op jit(solution)/shard_map/all_gather | solution.py:145
  15.9 313.9 %reduce-scatter.5.cloned.1.call-start = ((), (), s32[]{:S(2)}) async-start(), calls=%async_computation.6 | async-start | bytes 4718592 | tf_op jit(solution)/shard_map/reduce_scatter | solution.py:170
  87.2 7.6 %copy-start.5 = (f32[1024,64]{0,1:T(8,128)S(1)}, f32[1024,64]{0,1:T(8,128)}, u32[]{:S(2)}) copy-start(f32[1024,64]{0,1:T(8,128)} %get-tuple-element.64) | copy-start | bytes 786436
  159.0 4.6 %copy-start.12 = (bf16[1024,256]{0,1:T(8,128)(2,1)S(1)}, bf16[1024,256]{0,1:T(8,128)(2,1)}, u32[]{:S(2)}) copy-start(bf16[1024,256]{0,1:T(8,128)(2,1)} %convolution_convert_fusion.1) | copy-start | bytes 1572868
  230.7 7.7 %copy-start.6 = (f32[1024,64]{0,1:T(8,128)S(1)}, f32[1024,64]{0,1:T(8,128)}, u32[]{:S(2)}) copy-start(f32[1024,64]{0,1:T(8,128)} %get-tuple-element.64) | copy-start | bytes 786436
  230.7 7.7 %copy-start.8 = (f32[1024,2,128]{0,2,1:T(8,128)S(1)}, f32[1024,2,128]{0,2,1:T(8,128)}, u32[]{:S(2)}) copy-start(f32[1024,2,128]{0,2,1:T(8,128)} %fusion.34) | copy-start | bytes 3145732
  230.7 7.7 %copy-start.9 = (f32[1024,2,128]{0,2,1:T(8,128)S(1)}, f32[1024,2,128]{0,2,1:T(8,128)}, u32[]{:S(2)}) copy-start(f32[1024,2,128]{0,2,1:T(8,128)} %fusion.31) | copy-start | bytes 3145732
  241.5 1.4 copy-start.10
  242.9 3.5 copy-start.13
  242.9 3.5 copy-start.14
  242.9 3.5 copy-start.15
  243.0 3.5 copy-start.16
  246.4 171.2 %reduce-scatter.3.cloned.1.call-start = ((), (), s32[]{:S(2)}) async-start(), calls=%async_computation.3 | async-start | bytes 4718592 | tf_op jit(solution)/shard_map/reduce_scatter | solution.py:162
  251.7 5.0 %copy-start.18 = (f32[2,1024,1024]{1,2,0:T(8,128)S(1)}, f32[2,1024,1024]{1,2,0:T(8,128)}, u32[]{:S(2)}) copy-start(f32[2,1024,1024]{1,2,0:T(8,128)} %get-tuple-element.68) | copy-start | bytes 25165828
  257.4 72.3 %copy-start.1 = (f32[1,128,2048]{2,1,0:T(8,128)S(1)}, f32[1,128,2048]{2,1,0:T(8,128)}, u32[]{:S(2)}) copy-start(f32[1,128,2048]{2,1,0:T(8,128)} %param.9) | copy-start | bytes 3145732
  257.4 72.3 %copy-start.17 = (f32[1,2048]{1,0:T(1,128)S(1)}, f32[1,2048]{1,0:T(1,128)}, u32[]{:S(2)}) copy-start(f32[1,2048]{1,0:T(1,128)} %param.11) | copy-start | bytes 24580
  257.9 159.7 %copy-start.2 = (f32[1,128,2048]{2,1,0:T(8,128)S(1)}, f32[1,128,2048]{2,1,0:T(8,128)}, u32[]{:S(2)}) copy-start(f32[1,128,2048]{2,1,0:T(8,128)} %param.8) | copy-start | bytes 3145732
  333.6 85.3 %collective-permute-start.1 = (bf16[128,2048]{1,0:T(8,128)(2,1)}, bf16[128,2048]{1,0:T(8,128)(2,1)S(1)}, u32[]{:S(2)}, u32[]{:S(2)}) collective-permute-start(bf16[128,2048]{1,0:T(8,128)(2,1)} %fusion.43), channel_id=1, source_target_pairs={{0,120},{8,0},{16,8},{24,16},{32,24},{40,32},{48,40},{56,48},{64,5... | collective-permute-start | bytes 1572872 | tf_op jit(solution)/shard_map/ppermute | solution.py:12
  418.7 10.8 %collective-permute-start = (bf16[128,2048]{1,0:T(8,128)(2,1)S(1)}, bf16[128,2048]{1,0:T(8,128)(2,1)S(1)}, u32[]{:S(2)}, u32[]{:S(2)}) collective-permute-start(bf16[128,2048]{1,0:T(8,128)(2,1)S(1)} %fusion.56), channel_id=1, source_target_pairs={{0,8},{8,16},{16,24},{24,32},{32,40},{40,48},{48,56},{56,64},{64,7... | collective-permute-start | bytes 1572872 | tf_op jit(solution)/shard_map/ppermute | solution.py:12
  (2 other events, 2.0 us)
Sparse Core Ops, SparseCore 0:
  13.1 74.0 all-gather.5
  89.5 69.4 all-gather.7
  161.3 69.3 all-gather.3
  246.5 83.1 reduce-scatter.4
  333.5 84.0 reduce-scatter.2
where the time goes:
time: 438 us; the launch traced here: 437 us
  waiting for transfers between devices  306 us (70%)
  matrix products  90.4 us (21%)
  other arithmetic  19.9 us (5%)
  between operations  14.1 us (3%)
  local copies, waits for them, and re-layouts  5.42 us (1%)
    reduce_scatter x1, waiting for transfers between devices, shards(): lax.psum_scatter(times_t(attn, w_out[0]).astype(jnp.bfloat16), 'seq', sca...  83.1 us
    reduce_scatter x1, waiting for transfers between devices, shards(): lax.psum_scatter((times_t(query_grad, w_query[0]) + times_t(key_grad, w_k...  68.6 us
    all_gather x1, waiting for transfers between devices, shards(): all_bwd = lax.all_gather(normed_bwd, 'seq', axis=0, tiled=True)  66.6 us
    all_gather x1, waiting for transfers between devices, shards(): all_grad = lax.all_gather(grad_low, 'seq', axis=0, tiled=True)  51.2 us
    all_gather x1, waiting for transfers between devices, shards(): all_fwd = lax.all_gather(normed_fwd, 'seq', axis=0, tiled=True)  26.3 us
    dot_general x1, matrix products, step(): jnp.einsum('hqk,qhd->khd', score_grad, query_block, preferred_element_typ...  15.4 us
    dot_general x1, matrix products, step(): jnp.einsum('hqk,khd->qhd', score_grad, key_heads, preferred_element_type=...  14.9 us
    ppermute x2, waiting for transfers between devices, passed_along(): return lax.ppermute(value, axis, pairs)  9.62 us
  transfers between devices with their start and end apart: 7, of which 6 were waited for; matrix products, arithmetic and copies ran while one was open for 21% of the time, Pallas kernels for 0%

commit v1 on v0

--- a/solution.py
+++ b/solution.py
@@ -2,6 +2,7 @@
 import jax.numpy as jnp
 from jax import lax
 from jax.sharding import PartitionSpec as P
+from jax.lax import all_to_all, axis_size
 
 HD = 128
 
@@ -143,7 +144,13 @@
     grad_low = grad.astype(jnp.bfloat16)
     full_cos, full_sin = rope_tables(jnp.arange(length))
     all_fwd = lax.all_gather(normed_fwd, "seq", axis=0, tiled=True)
-    all_bwd = lax.all_gather(normed_bwd, "seq", axis=0, tiled=True)
+    tell_lines = lambda my_tile, mesh_dim: jnp.concatenate(
+        all_to_all(
+            jnp.stack([my_tile for _ in range(axis_size(mesh_dim))], axis=0), mesh_dim, 0, 0
+        ),
+        axis=0,
+    )
+    all_bwd = tell_lines(normed_bwd, "seq")
     all_grad = lax.all_gather(grad_low, "seq", axis=0, tiled=True)
 
     def project(normed):

time: 438 us -> 392 us (0.89)
  waiting for transfers between devices: 306 us -> 252 us
  starting transfers between devices: 1.17 us -> 8.18 us
    all_gather x1 -> x0, waiting for transfers between devices: 66.6 us -> none  [shards(): all_bwd = lax.all_gather(normed_bwd, 'seq', axis=0, tiled=True)]
    all_to_all x0 -> x1, waiting for transfers between devices: none -> 63.6 us  [shards(): all_to_all(jnp.stack([my_tile for _ in range(axis_size(mesh_dim))], axis=...]
    all_gather x1, waiting for transfers between devices: 51.2 us -> 0.93 us  [shards(): all_grad = lax.all_gather(grad_low, 'seq', axis=0, tiled=True)]
    all_to_all x0 -> x1, starting transfers between devices: none -> 7.04 us  [shards(): all_to_all(jnp.stack([my_tile for _ in range(axis_size(mesh_dim))], axis=...]
  transfers between devices with their start and end apart: 7 -> 7, of which waited for: 6 -> 6; matrix products, arithmetic and copies ran while one was open for 21% -> 25% of each run, Pallas kernels for 0% -> 0%
where the time goes in v1:
time: 392 us
  waiting for transfers between devices  252 us (64%)
  matrix products  90.7 us (23%)
  other arithmetic  18.2 us (5%)
  between operations  14.1 us (4%)
  local copies, waits for them, and re-layouts  8.64 us (2%)
  starting transfers between devices  8.18 us (2%)
    reduce_scatter x1, waiting for transfers between devices, shards(): lax.psum_scatter(times_t(attn, w_out[0]).astype(jnp.bfloat16), 'seq', sca...  83.1 us
    reduce_scatter x1, waiting for transfers between devices, shards(): lax.psum_scatter((times_t(query_grad, w_query[0]) + times_t(key_grad, w_k...  68.5 us
    all_to_all x1, waiting for transfers between devices, shards(): all_to_all(jnp.stack([my_tile for _ in range(axis_size(mesh_dim))], axis=...  63.6 us
    all_gather x1, waiting for transfers between devices, shards(): all_fwd = lax.all_gather(normed_fwd, 'seq', axis=0, tiled=True)  26.3 us
    dot_general x1, matrix products, step(): jnp.einsum('hqk,qhd->khd', score_grad, query_block, preferred_element_typ...  15.5 us
    dot_general x1, matrix products, step(): jnp.einsum('hqk,khd->qhd', score_grad, key_heads, preferred_element_type=...  15 us
    ppermute x2, waiting for transfers between devices, passed_along(): return lax.ppermute(value, axis, pairs)  9.62 us
    dot_general x4, matrix products, times_t(): lax.dot_general(left, right, (((1,), (1,)), ((), ())), preferred_element_...  9.26 us
  transfers between devices with their start and end apart: 7, of which 6 were waited for; matrix products, arithmetic and copies ran while one was open for 25% of the time, Pallas kernels for 0%

profile of v1, /device:TPU:0, one launch (start us, length us, event | category | flops | bytes accessed | tf_op | source)
XLA Modules:
  0.0 391.8 jit_solution(2905522748718804234)
XLA Ops:
  12.3 2.5 stack.5
  14.8 7.0 %all-to-all-start = ((bf16[8,128,2048]{2,1,0:T(8,128)(2,1)}), bf16[8,128,2048]{2,1,0:T(8,128)(2,1)}, u32[]{:S(2)}, u32[]{:S(2)}) async-start(bf16[8,128,2048]{2,1,0:T(8,128)(2,1)} %stack.5), calls=%async_computation.1 | async-start | bytes 8388608 | tf_op jit(solution)/shard_map/all_to_all | solution.py:148
  24.5 2.3 copy.34
  28.6 63.6 %all-to-all-done = bf16[8,128,2048]{2,1,0:T(8,128)(2,1)} async-done(((bf16[8,128,2048]{2,1,0:T(8,128)(2,1)}), bf16[8,128,2048]{2,1,0:T(8,128)(2,1)}, u32[]{:S(2)}, u32[]{:S(2)}) %all-to-all-start) | async-done | bytes 4194336 | tf_op jit(solution)/shard_map/all_to_all | solution.py:148
  92.2 3.8 fusion.84
  96.0 3.8 fusion.83
  101.2 7.2 %fusion.81 = (f32[2,1024]{1,0:T(2,128)S(1)}, f32[2,1024,1024]{1,2,0:T(8,128)}) fusion(bf16[1024,2,64]{0,2,1:T(8,128)(2,1)} %get-tuple-element.38, bf16[1024,2,64]{0,2,1:T(8,128)(2,1)} %get-tuple-element.37, bf16[1024,2,64]{0,2,1:T(8,128)(2,1)} %get-tuple-element.59, bf16[1024,2,64]{0,2,1:T(8,128)(2,1)} %get-tuple-element.60), kind=kOutput, calls=%fused_computation.108 | convolution fusion | flops 545260544 | bytes 9445376 | tf_op jit(solution)/shard_map/while/body/eval_jaxpr/sub | solution.py:104
  108.4 4.3 %convolution_convert_fusion.1 = bf16[1024,256]{0,1:T(8,128)(2,1)} fusion(bf16[1024,2048]{1,0:T(8,128)(2,1)} %bitcast.16, bf16[1,2048,256]{2,1,0:T(8,128)(2,1)S(1)} %copy-done), kind=kOutput, calls=%fused_computation.31 | convolution fusion | flops 1074003968 | bytes 5767168 | tf_op jit(solution)/shard_map/dot_general | solution.py:163
  113.6 3.8 convolution_convert_fusion.2
  118.3 4.5 %fusion.85 = f32[2,1024,1024]{1,2,0:T(8,128)} fusion(bf16[1024,2,128]{0,2,1:T(8,128)(2,1)S(1)} %bitcast.118, bf16[1024,2,128]{0,2,1:T(8,128)(2,1)S(1)} %bitcast.120), kind=kOutput, calls=%fused_computation.112 | convolution fusion | flops 536870912 | bytes 9437184 | tf_op jit(solution)/shard_map/while/body/eval_jaxpr/qhd,khd->hqk/dot_general | solution.py:111
  122.8 15.5 %fusion.30 = f32[1024,2,128]{0,2,1:T(8,128)} fusion(f32[2,1024,1024]{1,2,0:T(8,128)} %fusion.85, bf16[1024,2,64]{0,2,1:T(8,128)(2,1)} %get-tuple-element.38, bf16[1024,2,64]{0,2,1:T(8,128)(2,1)} %get-tuple-element.37, f32[2,1024,1024]{1,2,0:T(8,128)} %get-tuple-element.64, f32[2,1024]{1,0:T(2,128)S(1)} %get-tuple-element.63), kind=kOutput, calls=%fused_computation.28 | convolution fusion | flops 552602624 | bytes 18358272 | tf_op jit(solution)/shard_map/while/body/eval_jaxpr/hqk,qhd->khd/dot_general | solution.py:119
  138.3 15.0 %fusion.27 = f32[1024,2,128]{0,2,1:T(8,128)} fusion(f32[2,1024,1024]{1,2,0:T(8,128)} %fusion.85, bf16[1024,2,64]{0,2,1:T(8,128)(2,1)} %get-tuple-element.59, bf16[1024,2,64]{0,2,1:T(8,128)(2,1)} %get-tuple-element.60, f32[2,1024,1024]{1,2,0:T(8,128)} %get-tuple-element.64, f32[2,1024]{1,0:T(2,128)S(1)} %get-tuple-element.63), kind=kOutput, calls=%fused_computation.27 | convolution fusion | flops 552602624 | bytes 18358272 | tf_op jit(solution)/shard_map/while/body/eval_jaxpr/hqk,khd->qhd/dot_general | solution.py:116
  153.3 5.9 %fusion.34 = bf16[2,128,1024]{2,1,0:T(8,128)(2,1)} fusion(bf16[1024,2,128]{0,2,1:T(8,128)(2,1)} %bitcast.119, f32[2,1024,1024]{1,2,0:T(8,128)} %get-tuple-element.64, f32[2,1024]{1,0:T(2,128)S(1)} %get-tuple-element.63), kind=kOutput, calls=%fused_computation.30 | convolution fusion | flops 541327360 | bytes 9445376 | tf_op jit(solution)/shard_map/while/body/eval_jaxpr/hqk,qhd->khd/dot_general | solution.py:105
  159.2 26.3 %all-gather.3.cloned.1.call-done = bf16[1024,2048]{1,0:T(8,128)(2,1)} async-done(((bf16[128,2048]{1,0:T(8,128)(2,1)}), bf16[1024,2048]{1,0:T(8,128)(2,1)}) %all-gather.3.cloned.1.call-update) | async-done | bytes 4194320 | tf_op jit(solution)/shard_map/all_gather | solution.py:146
  185.5 3.9 fusion.12
  189.4 3.8 fusion.14
  197.7 3.4 add_convert_fusion
  201.2 5.2 %fusion.82 = (f32[2,1024]{1,0:T(2,128)S(1)}, f32[2,1024,1024]{1,2,0:T(8,128)}) fusion(bf16[1024,2,64]{0,2,1:T(8,128)(2,1)S(1)} %copy-done.13, bf16[1024,2,64]{0,2,1:T(8,128)(2,1)S(1)} %copy-done.14, bf16[1024,2,64]{0,2,1:T(8,128)(2,1)S(1)} %copy-done.15, bf16[1024,2,64]{0,2,1:T(8,128)(2,1)S(1)} %copy-done.16), kind=kOutput, calls=%fused_computation.109 | convolution fusion | flops 545260544 | bytes 9445376 | tf_op jit(solution)/shard_map/while/body/eval_jaxpr/sub | solution.py:78
  206.4 3.9 convolution_convert_fusion.3
  212.7 3.2 convolution_convert_fusion
  216.0 68.5 %reduce-scatter.5.cloned.1.call-done = bf16[128,2048]{1,0:T(8,128)(2,1)} async-done(((bf16[1024,2048]{1,0:T(8,128)(2,1)}), bf16[128,2048]{1,0:T(8,128)(2,1)}) %reduce-scatter.5.cloned.1.call-update) | async-done | bytes 524304 | tf_op jit(solution)/shard_map/reduce_scatter | solution.py:177
  285.7 2.5 fusion.43
  289.1 83.1 %reduce-scatter.3.cloned.1.call-done = bf16[128,2048]{1,0:T(8,128)(2,1)} async-done(((bf16[1024,2048]{1,0:T(8,128)(2,1)}), bf16[128,2048]{1,0:T(8,128)(2,1)}) %reduce-scatter.3.cloned.1.call-update) | async-done | bytes 524304 | tf_op jit(solution)/shard_map/reduce_scatter | solution.py:169
  374.6 9.6 %collective-permute-done = bf16[128,2048]{1,0:T(8,128)(2,1)S(1)} collective-permute-done((bf16[128,2048]{1,0:T(8,128)(2,1)S(1)}, bf16[128,2048]{1,0:T(8,128)(2,1)S(1)}, u32[]{:S(2)}, u32[]{:S(2)}) %collective-permute-start) | collective-permute-done | bytes 524320 | tf_op jit(solution)/shard_map/ppermute | solution.py:13
  (72 shorter events, 25.1 us)
Async XLA Ops:
  7.2 101.2 %copy-start = (bf16[1,2048,256]{2,1,0:T(8,128)(2,1)S(1)}, bf16[1,2048,256]{2,1,0:T(8,128)(2,1)}, u32[]{:S(2)}) copy-start(bf16[1,2048,256]{2,1,0:T(8,128)(2,1)} %param.14) | copy-start | bytes 3145732
  7.2 106.5 %all-gather.5.cloned.1.call-start = ((), (), s32[]{:S(2)}) async-start(), calls=%async_computation.5 | async-start | bytes 4718592 | tf_op jit(solution)/shard_map/all_gather | solution.py:154
  9.4 12.5 %copy-start.2 = (f32[1,128,2048]{2,1,0:T(8,128)S(1)}, f32[1,128,2048]{2,1,0:T(8,128)}, u32[]{:S(2)}) copy-start(f32[1,128,2048]{2,1,0:T(8,128)} %param.8) | copy-start | bytes 3145732
  9.4 12.6 %copy-start.17 = (f32[1,2048]{1,0:T(1,128)S(1)}, f32[1,2048]{1,0:T(1,128)}, u32[]{:S(2)}) copy-start(f32[1,2048]{1,0:T(1,128)} %param.11) | copy-start | bytes 24580
  12.3 10.8 %copy-start.3 = (bf16[1,2048,256]{2,1,0:T(8,128)(2,1)S(1)}, bf16[1,2048,256]{2,1,0:T(8,128)(2,1)}, u32[]{:S(2)}) copy-start(bf16[1,2048,256]{2,1,0:T(8,128)(2,1)} %param.13) | copy-start | bytes 3145732
  14.8 77.4 %all-to-all-start = ((bf16[8,128,2048]{2,1,0:T(8,128)(2,1)}), bf16[8,128,2048]{2,1,0:T(8,128)(2,1)}, u32[]{:S(2)}, u32[]{:S(2)}) async-start(bf16[8,128,2048]{2,1,0:T(8,128)(2,1)} %stack.5), calls=%async_computation.1 | async-start | bytes 8388608 | tf_op jit(solution)/shard_map/all_to_all | solution.py:148
  21.8 163.6 %all-gather.3.cloned.1.call-start = ((), (), s32[]{:S(2)}) async-start(), calls=%async_computation.3 | async-start | bytes 4718592 | tf_op jit(solution)/shard_map/all_gather | solution.py:146
  23.0 261.4 %reduce-scatter.5.cloned.1.call-start = ((), (), s32[]{:S(2)}) async-start(), calls=%async_computation.6 | async-start | bytes 4718592 | tf_op jit(solution)/shard_map/reduce_scatter | solution.py:177
  92.2 7.6 %copy-start.5 = (f32[1024,64]{0,1:T(8,128)S(1)}, f32[1024,64]{0,1:T(8,128)}, u32[]{:S(2)}) copy-start(f32[1024,64]{0,1:T(8,128)} %get-tuple-element.62) | copy-start | bytes 786436
  113.6 4.7 %copy-start.12 = (bf16[1024,256]{0,1:T(8,128)(2,1)S(1)}, bf16[1024,256]{0,1:T(8,128)(2,1)}, u32[]{:S(2)}) copy-start(bf16[1024,256]{0,1:T(8,128)(2,1)} %convolution_convert_fusion.1) | copy-start | bytes 1572868
  185.4 7.7 %copy-start.6 = (f32[1024,64]{0,1:T(8,128)S(1)}, f32[1024,64]{0,1:T(8,128)}, u32[]{:S(2)}) copy-start(f32[1024,64]{0,1:T(8,128)} %get-tuple-element.62) | copy-start | bytes 786436
  185.4 7.7 %copy-start.8 = (f32[1024,2,128]{0,2,1:T(8,128)S(1)}, f32[1024,2,128]{0,2,1:T(8,128)}, u32[]{:S(2)}) copy-start(f32[1024,2,128]{0,2,1:T(8,128)} %fusion.30) | copy-start | bytes 3145732
  185.5 7.7 %copy-start.9 = (f32[1024,2,128]{0,2,1:T(8,128)S(1)}, f32[1024,2,128]{0,2,1:T(8,128)}, u32[]{:S(2)}) copy-start(f32[1024,2,128]{0,2,1:T(8,128)} %fusion.27) | copy-start | bytes 3145732
  194.9 1.4 copy-start.4
  196.3 1.3 copy-start.10
  197.7 3.5 copy-start.13
  197.7 3.5 copy-start.14
  197.7 3.5 copy-start.15
  197.7 3.5 copy-start.16
  201.1 171.1 %reduce-scatter.3.cloned.1.call-start = ((), (), s32[]{:S(2)}) async-start(), calls=%async_computation.4 | async-start | bytes 4718592 | tf_op jit(solution)/shard_map/reduce_scatter | solution.py:169
  206.4 5.0 %copy-start.18 = (f32[2,1024,1024]{1,2,0:T(8,128)S(1)}, f32[2,1024,1024]{1,2,0:T(8,128)}, u32[]{:S(2)}) copy-start(f32[2,1024,1024]{1,2,0:T(8,128)} %get-tuple-element.66) | copy-start | bytes 25165828
  212.2 72.2 %copy-start.1 = (f32[1,128,2048]{2,1,0:T(8,128)S(1)}, f32[1,128,2048]{2,1,0:T(8,128)}, u32[]{:S(2)}) copy-start(f32[1,128,2048]{2,1,0:T(8,128)} %param.9) | copy-start | bytes 3145732
  288.2 85.3 %collective-permute-start.1 = (bf16[128,2048]{1,0:T(8,128)(2,1)}, bf16[128,2048]{1,0:T(8,128)(2,1)S(1)}, u32[]{:S(2)}, u32[]{:S(2)}) collective-permute-start(bf16[128,2048]{1,0:T(8,128)(2,1)} %fusion.43), channel_id=1, source_target_pairs={{0,120},{8,0},{16,8},{24,16},{32,24},{40,32},{48,40},{56,48},{64,5... | collective-permute-start | bytes 1572872 | tf_op jit(solution)/shard_map/ppermute | solution.py:13
  373.4 10.8 %collective-permute-start = (bf16[128,2048]{1,0:T(8,128)(2,1)S(1)}, bf16[128,2048]{1,0:T(8,128)(2,1)S(1)}, u32[]{:S(2)}, u32[]{:S(2)}) collective-permute-start(bf16[128,2048]{1,0:T(8,128)(2,1)S(1)} %fusion.57), channel_id=1, source_target_pairs={{0,8},{8,16},{16,24},{24,32},{32,40},{40,48},{48,56},{56,64},{64,7... | collective-permute-start | bytes 1572872 | tf_op jit(solution)/shard_map/ppermute | solution.py:13
  (2 other events, 2.0 us)
Sparse Core Ops, SparseCore 0:
  10.3 103.2 all-gather.4
  116.0 69.4 all-gather.2
  201.2 83.1 reduce-scatter.4
  288.2 84.0 reduce-scatter.2
